TPU v7x, 32 devices: a whole 2x2x4 slice. The times are simulated.
32 devices in a mesh: pipe: 4 (over x, core), expert: 4 (over z), tensor: 2 (over y).
Axes of the slice: x: 2, y: 2, z: 4, core: 2. Of those that a mesh axis runs over, the one named last changes fastest.
Arguments:
- stream: bfloat16 [2, 4, 64, 7168], P(None, 'pipe', 'expert', 'tensor'), may hold values from -6 to 6
- expert_ids: int32 [2, 4, 64, 2], P(None, 'pipe', 'expert'), may hold values from 0 to 3, all different within a row; in each aligned block of 16 rows (0 to 15, 16 to 31, ..., all dimensions but the last counted through in order) at most 12 rows name the same one
- norm_gain: float32 [4, 7168], P('pipe', 'tensor'), may hold values from 0.1 to 1.9
- router: float32 [4, 7168, 4], P('pipe', 'tensor'), may hold values from -0.0625 to 0.0625
- w_up: bfloat16 [4, 7168, 1024], P('expert', 'tensor'), may hold values from -0.0625 to 0.0625
- w_down: bfloat16 [4, 1024, 7168], P('expert', None, 'tensor'), may hold values from -0.1875 to 0.1875
Outputs:
- result: bfloat16 [2, 4, 64, 7168], P(None, 'pipe', 'expert', 'tensor')
Inputs may be any that keep to these rules, and one draw needn't show every extreme that they name: `expert_ids`: each token names 2 different experts. Among the 16 tokens of one direction held by one index of the expert axis at one section, at most 12 name any one expert, and in every draw some expert is named by exactly 12 of them.
All inputs are finite; a program needn't handle non-finite values.
Results may differ from a plain program's by a relative error of at most 0.0065.
Values may be sent and summed in bfloat16 or wider, within the bound.
A program may use at most 64 MiB of HBM per device.

v0:
```python
import jax
import jax.numpy as jnp
from jax import lax
from jax.sharding import PartitionSpec as P

norm_eps = 1e-06
route_scale = 2.5


def shifted(x, axis, by):
    size = lax.axis_size(axis)
    return lax.ppermute(x, axis, [(i, (i + by) % size) for i in range(size)])


def shards(stream, expert_ids, norm_gain, router, w_up, w_down):
    ahead = shifted(stream[0], "pipe", 1)
    behind = shifted(stream[1], "pipe", -1)
    arrived = jnp.concatenate([ahead, behind], axis=0).astype(jnp.float32)
    tok_rows = arrived.shape[1]
    quarter = arrived.shape[2]
    width = float(quarter * lax.axis_size("tensor"))
    scaled = arrived * norm_gain[0]
    squares = jnp.sum(arrived * arrived, axis=-1)
    highest = lax.Precision.HIGHEST
    total_sq = lax.psum(squares, "tensor")
    inverse = lax.rsqrt(total_sq / width + norm_eps)
    normed = scaled * inverse[..., None]
    logits = lax.psum(jnp.einsum("dtc,ce->dte", normed, router[0], precision=highest), "tensor")
    chosen = expert_ids[:, 0]
    fanout = chosen.shape[2]
    experts = router.shape[2]
    capacity = 3 * tok_rows * fanout // (2 * experts)
    picked = jnp.take_along_axis(logits, chosen, axis=-1)
    scores = jax.nn.sigmoid(picked)
    gates = route_scale * scores / jnp.sum(scores, axis=-1, keepdims=True)
    onehot = (chosen[..., None] == jnp.arange(experts, dtype=jnp.int32)).astype(jnp.int32)
    onehot = onehot.reshape(2, tok_rows * fanout, experts)
    earlier = jnp.cumsum(onehot, axis=1) - onehot
    within = jnp.sum(earlier * onehot, axis=-1).reshape(chosen.shape)
    heading = lax.broadcasted_iota(jnp.int32, chosen.shape, 0)
    member = lax.broadcasted_iota(jnp.int32, chosen.shape, 1)
    target = chosen * (2 * capacity) + heading * capacity + within
    anchor = heading * tok_rows + member
    owner = (
        jnp.full((experts * 2 * capacity,), 2 * tok_rows, jnp.int32)
        .at[target.reshape(-1)]
        .set(anchor.reshape(-1))
    )
    hidden = normed.astype(jnp.bfloat16).reshape(2 * tok_rows, quarter)
    table = jnp.concatenate([hidden, jnp.zeros((1, quarter), jnp.bfloat16)], axis=0)
    outgoing = table[owner].reshape(experts, 2 * capacity, quarter)
    upper = w_up[0]
    lower = w_down[0]
    received = lax.all_to_all(outgoing, "expert", split_axis=0, concat_axis=0, tiled=True)
    senders = received.shape[0]
    count = received.shape[1]
    inner = jnp.dot(received.reshape(-1, quarter), upper, preferred_element_type=jnp.float32)
    share = lax.psum_scatter(inner, "tensor", scatter_dimension=1, tiled=True)
    active = lax.all_gather(jax.nn.silu(share).astype(jnp.bfloat16), "tensor", axis=1, tiled=True)
    produced = jnp.dot(active, lower, preferred_element_type=jnp.float32).astype(jnp.bfloat16)
    answers = lax.all_to_all(
        produced.reshape(senders, count, quarter), "expert", split_axis=0, concat_axis=0, tiled=True
    )
    flat_back = answers.reshape(experts * 2 * capacity, quarter)
    gathered = (
        flat_back[target.reshape(-1)].reshape(2, tok_rows, fanout, quarter).astype(jnp.float32)
    )
    mixed = jnp.einsum("dtk,dtkc->dtc", gates, gathered)
    result = (arrived + mixed).astype(jnp.bfloat16)
    return result[:, None]


def solution(mesh):
    return jax.shard_map(
        shards,
        mesh=mesh,
        in_specs=(
            P(None, "pipe", "expert", "tensor"),
            P(None, "pipe", "expert", None),
            P("pipe", "tensor"),
            P("pipe", "tensor", None),
            P("expert", "tensor", None),
            P("expert", None, "tensor"),
        ),
        out_specs=P(None, "pipe", "expert", "tensor"),
        check_vma=False,
    )
```

profile of v0, /device:TPU:0, one launch (start us, length us, event | category | flops | bytes accessed | tf_op | source)
XLA Modules:
  0.0 101.9 jit_solution(15306226972587400173)
XLA Ops:
  6.5 0.0 copy-start
  6.5 1.0 slice_bitcast_fusion.1
  7.5 0.5 collective-permute-start
  8.1 2.0 %collective-permute-start.1 = (bf16[1,16,3584]{2,1,0:T(8,128)(2,1)S(1)}, bf16[1,16,3584]{2,1,0:T(8,128)(2,1)S(1)}, u32[]{:S(2)}, u32[]{:S(2)}) collective-permute-start(bf16[1,16,3584]{2,1,0:T(8,128)(2,1)S(1)} %get-tuple-element.8), channel_id=1, source_target_pairs={{0,24},{8,0},{16,8},{24,16},{1,25},{9,1},{17,9},{25,17},{2,26},{10... | collective-permute-start | bytes 344072 | tf_op jit(solution)/shard_map/ppermute | solution.py:12
  10.0 0.8 copy.14
  10.8 0.7 broadcast_multiply_fusion
  11.5 0.1 eq.16
  11.6 0.1 fusion.18
  11.7 0.1 reduce_window_sum.11
  11.7 0.2 select_reduce_fusion
  11.9 0.1 reshape.116
  12.0 0.1 copy.13
  12.1 0.1 mul.92
  12.2 0.1 iota.24
  12.3 0.1 iota.25
  12.4 0.1 iota_add_fusion
  12.5 0.1 reshape.149
  12.6 0.8 scatter_custom_fusion
  13.4 0.8 reduce
  14.1 0.0 collective-permute-done
  14.2 0.0 collective-permute-done.1
  14.2 0.1 multiply_reduce_fusion
  14.3 5.2 %psum.14 = f32[2,16]{1,0:T(2,128)S(1)} all-reduce(f32[2,16]{1,0:T(2,128)S(1)} %multiply_reduce_fusion), channel_id=1, replica_groups=mesh['pipe'=4,'expert'=4,'tensor'=2] {'tensor'}, use_global_device_ids=true, to_apply=%region_1.0 | all-reduce | flops 32 | bytes 256 | tf_op jit(solution)/shard_map/psum | solution.py:25
  19.5 0.1 mul.87
  19.6 0.1 fusion.9
  19.7 1.0 gather_fusion
  20.7 22.2 %all_to_all.10 = bf16[4,24,3584]{2,1,0:T(8,128)(2,1)S(1)} all-to-all(bf16[4,24,3584]{2,1,0:T(8,128)(2,1)S(1)} %bitcast.63), channel_id=1, replica_groups=mesh['pipe'=4,'expert'=4,'tensor'=2] {'expert'}, dimensions={0} | all-to-all | bytes 1376256 | tf_op jit(solution)/shard_map/all_to_all | solution.py:54
  42.8 5.1 %fusion.2 = f32[96,1024]{1,0:T(8,128)} fusion(bf16[96,3584]{1,0:T(8,128)(2,1)S(1)} %bitcast.62, bf16[1,3584,1024]{2,1,0:T(8,128)(2,1)} %param.10), kind=kOutput, calls=%fused_computation.6 | convolution fusion | flops 704643072 | bytes 8421376 | tf_op jit(solution)/shard_map/dot_general | solution.py:57
  47.9 0.0 reduce-scatter.2.cloned.1.call-update
  48.0 11.9 %reduce-scatter.2.cloned.1.call-done = f32[96,512]{1,0:T(8,128)} async-done(((f32[96,1024]{1,0:T(8,128)}), f32[96,512]{1,0:T(8,128)}) %reduce-scatter.2.cloned.1.call-update) | async-done | bytes 196624 | tf_op jit(solution)/shard_map/reduce_scatter | solution.py:58
  59.9 1.0 multiply_convert_fusion
  60.9 5.3 %all_gather.3 = bf16[96,1024]{1,0:T(8,128)(2,1)S(1)} all-gather(bf16[96,512]{1,0:T(8,128)(2,1)S(1)} %multiply_convert_fusion), channel_id=1, replica_groups=mesh['pipe'=4,'expert'=4,'tensor'=2] {'tensor'}, dimensions={1}, use_global_device_ids=true | all-gather | bytes 294912 | tf_op jit(solution)/shard_map/all_gather | solution.py:59
  66.2 5.2 %fusion.4 = bf16[96,3584]{1,0:T(8,128)(2,1)} fusion(bf16[96,1024]{1,0:T(8,128)(2,1)S(1)} %all_gather.3, bf16[1,1024,3584]{2,1,0:T(8,128)(2,1)} %param.11), kind=kOutput, calls=%fused_computation.8 | convolution fusion | flops 704987136 | bytes 8224768 | tf_op jit(solution)/shard_map/dot_general | solution.py:60
  71.4 4.6 %all-to-all-start.1 = ((bf16[4,24,3584]{2,1,0:T(8,128)(2,1)}), bf16[4,24,3584]{2,1,0:T(8,128)(2,1)S(1)}, u32[]{:S(2)}, u32[]{:S(2)}) async-start(bf16[4,24,3584]{2,1,0:T(8,128)(2,1)} %bitcast.13), calls=%async_computation.2 | async-start | bytes 1376256 | tf_op jit(solution)/shard_map/all_to_all | solution.py:61
  76.0 0.0 copy-done.1
  76.0 0.1 copy.11
  76.1 0.1 reshape.139
  76.2 1.8 %fusion.10 = f32[2,16,4]{1,2,0:T(4,128)S(1)} fusion(f32[2,16]{1,0:T(2,128)S(1)} %add_rsqrt_fusion, f32[3584]{0:T(1024)S(1)} %reduce, f32[1,3584,4]{1,2,0:T(4,128)S(1)} %copy-done, bf16[1,16,3584]{2,1,0:T(8,128)(2,1)S(1)} %collective-permute-done.1, bf16[1,16,3584]{2,1,0:T(8,128)(2,1)S(1)} %collective-permute-done), kind=kOutput, calls=%fused_computation.14 | convolution fusion | flops 5963776 | bytes 301696 | tf_op jit(solution)/shard_map/dtc,ce->dte/dot_general | solution.py:28
  78.0 4.9 %psum.15 = f32[2,16,4]{1,2,0:T(4,128)S(1)} all-reduce(f32[2,16,4]{1,2,0:T(4,128)S(1)} %fusion.10), channel_id=1, replica_groups=mesh['pipe'=4,'expert'=4,'tensor'=2] {'tensor'}, use_global_device_ids=true, to_apply=%region_2.0 | all-reduce | flops 128 | bytes 1024 | tf_op jit(solution)/shard_map/psum | solution.py:28
  82.9 1.0 gather_fusion.2
  83.9 0.1 reshape.142
  84.0 0.1 copy.12
  84.2 0.1 copy.15
  84.3 8.4 %all-to-all-done.1 = bf16[4,24,3584]{2,1,0:T(8,128)(2,1)S(1)} async-done(((bf16[4,24,3584]{2,1,0:T(8,128)(2,1)}), bf16[4,24,3584]{2,1,0:T(8,128)(2,1)S(1)}, u32[]{:S(2)}, u32[]{:S(2)}) %all-to-all-start.1) | async-done | bytes 688160 | tf_op jit(solution)/shard_map/all_to_all | solution.py:61
  92.7 0.8 gather_fusion.1
  93.5 0.2 reshape.121
  93.7 0.6 fusion.27
  94.3 0.7 fusion.14
  (14 shorter events, 0.1 us)
Async XLA Ops:
  6.5 69.7 %copy-start = (f32[1,3584,4]{1,2,0:T(4,128)S(1)}, f32[1,3584,4]{1,2,0:T(4,128)}, u32[]{:S(2)}) copy-start(f32[1,3584,4]{1,2,0:T(4,128)} %param.9) | copy-start | bytes 172036
  6.5 53.3 %reduce-scatter.2.cloned.1.call-start = ((), (), s32[]{:S(2)}) async-start(), calls=%async_computation.3 | async-start | bytes 589824 | tf_op jit(solution)/shard_map/reduce_scatter | solution.py:58
  7.5 6.6 %collective-permute-start = (bf16[1,16,3584]{2,1,0:T(8,128)(2,1)S(1)}, bf16[1,16,3584]{2,1,0:T(8,128)(2,1)S(1)}, u32[]{:S(2)}, u32[]{:S(2)}) collective-permute-start(bf16[1,16,3584]{2,1,0:T(8,128)(2,1)S(1)} %get-tuple-element.7), channel_id=1, source_target_pairs={{0,8},{8,16},{16,24},{24,0},{1,9},{9,17},{17,25},{25,1},{2,10},{10... | collective-permute-start | bytes 344072 | tf_op jit(solution)/shard_map/ppermute | solution.py:12
  8.1 6.1 %collective-permute-start.1 = (bf16[1,16,3584]{2,1,0:T(8,128)(2,1)S(1)}, bf16[1,16,3584]{2,1,0:T(8,128)(2,1)S(1)}, u32[]{:S(2)}, u32[]{:S(2)}) collective-permute-start(bf16[1,16,3584]{2,1,0:T(8,128)(2,1)S(1)} %get-tuple-element.8), channel_id=1, source_target_pairs={{0,24},{8,0},{16,8},{24,16},{1,25},{9,1},{17,9},{25,17},{2,26},{10... | collective-permute-start | bytes 344072 | tf_op jit(solution)/shard_map/ppermute | solution.py:12
  66.1 9.9 %copy-start.1 = (s32[2,1,16,2]{2,3,1,0:T(2,128)S(1)}, s32[2,1,16,2]{2,3,1,0:T(2,128)}, u32[]{:S(2)}) copy-start(s32[2,1,16,2]{2,3,1,0:T(2,128)} %param.7) | copy-start | bytes 772
  71.4 21.3 %all-to-all-start.1 = ((bf16[4,24,3584]{2,1,0:T(8,128)(2,1)}), bf16[4,24,3584]{2,1,0:T(8,128)(2,1)S(1)}, u32[]{:S(2)}, u32[]{:S(2)}) async-start(bf16[4,24,3584]{2,1,0:T(8,128)(2,1)} %bitcast.13), calls=%async_computation.2 | async-start | bytes 1376256 | tf_op jit(solution)/shard_map/all_to_all | solution.py:61
Sparse Core Ops, SparseCore 0:
  48.1 11.7 reduce-scatter.1
where the time goes:
time: 102 us
  blocking collectives  37.5 us (37%)
  waiting for transfers between devices  20.4 us (20%)
  between operations  13.6 us (13%)
  matrix products  12.8 us (13%)
  starting transfers between devices  7.13 us (7%)
  local copies, waits for them, and re-layouts  6.7 us (7%)
  other arithmetic  3.87 us (4%)
    all_to_all x1, blocking collectives, shards(): lax.all_to_all(outgoing, 'expert', split_axis=0, concat_axis=0, tiled=True)  22.2 us
    reduce_scatter x1, waiting for transfers between devices, shards(): share = lax.psum_scatter(inner, 'tensor', scatter_dimension=1, tiled=True)  11.9 us
    all_to_all x1, waiting for transfers between devices, shards(): lax.all_to_all(produced.reshape(senders, count, quarter), 'expert', split...  8.42 us
    all_gather x1, blocking collectives, shards(): lax.all_gather(jax.nn.silu(share).astype(jnp.bfloat16), 'tensor', axis=1,...  5.29 us
    dot_general x1, matrix products, shards(): jnp.dot(active, lower, preferred_element_type=jnp.float32)  5.25 us
    psum x1, blocking collectives, shards(): total_sq = lax.psum(squares, 'tensor')  5.16 us
    dot_general x1, matrix products, shards(): jnp.dot(received.reshape(-1, quarter), upper, preferred_element_type=jnp....  5.11 us
    psum x1, blocking collectives, shards(): lax.psum(jnp.einsum('dtc,ce->dte', normed, router[0], precision=highest),...  4.93 us
  transfers between devices with their start and end apart: 4, of which 2 were waited for; matrix products, arithmetic and copies ran while one was open for 7% of the time, Pallas kernels for 0%

commit v1 on v0

--- a/solution.py
+++ b/solution.py
@@ -58,9 +58,19 @@
     share = lax.psum_scatter(inner, "tensor", scatter_dimension=1, tiled=True)
     active = lax.all_gather(jax.nn.silu(share).astype(jnp.bfloat16), "tensor", axis=1, tiled=True)
     produced = jnp.dot(active, lower, preferred_element_type=jnp.float32).astype(jnp.bfloat16)
-    answers = lax.all_to_all(
-        produced.reshape(senders, count, quarter), "expert", split_axis=0, concat_axis=0, tiled=True
-    )
+    shard = produced.reshape(senders, count, quarter)
+    ways, here = (lax.axis_size("expert"), lax.axis_index("expert"))
+    width_2 = shard.shape[0] // ways
+    lengths = list(shard.shape)
+    lengths[0] = width_2
+    height = lengths[0]
+    lengths[0] = height * ways
+    answers = jnp.zeros(lengths, shard.dtype)
+    for mask in range(ways):
+        part = lax.dynamic_slice_in_dim(shard, (here ^ mask) * width_2, width_2, axis=0)
+        if mask:
+            part = lax.ppermute(part, "expert", [(d, d ^ mask) for d in range(ways)])
+        answers = lax.dynamic_update_slice_in_dim(answers, part, (here ^ mask) * height, axis=0)
     flat_back = answers.reshape(experts * 2 * capacity, quarter)
     gathered = (
         flat_back[target.reshape(-1)].reshape(2, tok_rows, fanout, quarter).astype(jnp.float32)

time: 102 us -> 98.1 us (0.962)
  blocking collectives: 37.5 us -> 15.1 us
  waiting for transfers between devices: 20.4 us -> 33.6 us
  starting transfers between devices: 7.13 us -> 11.9 us
    all_to_all x1 -> x0, blocking collectives: 22.2 us -> none  [shards(): lax.all_to_all(outgoing, 'expert', split_axis=0, concat_axis=0, tiled=True)]
    ppermute x0 -> x3, waiting for transfers between devices: none -> 11.6 us  [shards(): part = lax.ppermute(part, 'expert', [(d, d ^ mask) for d in range(ways)])]
    all_to_all x1, waiting for transfers between devices: 8.42 us -> 17.3 us  [shards(): lax.all_to_all(outgoing, 'expert', split_axis=0, concat_axis=0, tiled=True)]
    reduce_scatter x1, waiting for transfers between devices: 11.9 us -> 4.23 us  [shards(): share = lax.psum_scatter(inner, 'tensor', scatter_dimension=1, tiled=True)]
    ppermute x0 -> x3, starting transfers between devices: none -> 4.52 us  [shards(): part = lax.ppermute(part, 'expert', [(d, d ^ mask) for d in range(ways)])]
  transfers between devices with their start and end apart: 4 -> 7, of which waited for: 2 -> 5; matrix products, arithmetic and copies ran while one was open for 7% -> 8% of each run, Pallas kernels for 0% -> 0%
where the time goes in v1:
time: 98.1 us; the launch traced here: 97.7 us
  waiting for transfers between devices  33.6 us (34%)
  blocking collectives  15.1 us (15%)
  between operations  13.6 us (14%)
  starting transfers between devices  11.9 us (12%)
  matrix products  11.9 us (12%)
  local copies, waits for them, and re-layouts  7.72 us (8%)
  other arithmetic  3.87 us (4%)
    all_to_all x1, waiting for transfers between devices, shards(): lax.all_to_all(outgoing, 'expert', split_axis=0, concat_axis=0, tiled=True)  17.3 us
    ppermute x3, waiting for transfers between devices, shards(): part = lax.ppermute(part, 'expert', [(d, d ^ mask) for d in range(ways)])  11.6 us
    all_gather x1, blocking collectives, shards(): lax.all_gather(jax.nn.silu(share).astype(jnp.bfloat16), 'tensor', axis=1,...  5.29 us
    dot_general x1, matrix products, shards(): jnp.dot(received.reshape(-1, quarter), upper, preferred_element_type=jnp....  5.13 us
    psum x1, blocking collectives, shards(): lax.psum(jnp.einsum('dtc,ce->dte', normed, router[0], precision=highest),...  4.93 us
    psum x1, blocking collectives, shards(): total_sq = lax.psum(squares, 'tensor')  4.92 us
    all_to_all x1, starting transfers between devices, shards(): lax.all_to_all(outgoing, 'expert', split_axis=0, concat_axis=0, tiled=True)  4.87 us
    ppermute x3, starting transfers between devices, shards(): part = lax.ppermute(part, 'expert', [(d, d ^ mask) for d in range(ways)])  4.52 us
  transfers between devices with their start and end apart: 7, of which 5 were waited for; matrix products, arithmetic and copies ran while one was open for 8% of the time, Pallas kernels for 0%

profile of v1, /device:TPU:0, one launch (start us, length us, event | category | flops | bytes accessed | tf_op | source)
XLA Modules:
  0.0 97.7 jit_solution(7329529562692589962)
XLA Ops:
  6.5 1.0 slice_bitcast_fusion.1
  7.5 2.5 %collective-permute-start.1 = (bf16[1,16,3584]{2,1,0:T(8,128)(2,1)S(1)}, bf16[1,16,3584]{2,1,0:T(8,128)(2,1)S(1)}, u32[]{:S(2)}, u32[]{:S(2)}) collective-permute-start(bf16[1,16,3584]{2,1,0:T(8,128)(2,1)S(1)} %get-tuple-element.12), channel_id=1, source_target_pairs={{0,24},{8,0},{16,8},{24,16},{1,25},{9,1},{17,9},{25,17},{2,26},{10... | collective-permute-start | bytes 344072 | tf_op jit(solution)/shard_map/ppermute | solution.py:12
  10.0 0.8 copy.14
  10.7 0.7 broadcast_multiply_fusion
  11.4 0.1 eq.16
  11.5 0.1 fusion.18
  11.6 0.1 reduce_window_sum.11
  11.7 0.2 select_reduce_fusion
  11.8 0.1 reshape.116
  11.9 0.1 copy.13
  12.0 0.1 mul.92
  12.1 0.1 iota.24
  12.2 0.1 iota.25
  12.3 0.1 iota_add_fusion
  12.4 0.1 reshape.149
  12.5 0.8 scatter_custom_fusion
  13.3 0.8 reduce
  14.1 0.5 collective-permute-done
  14.5 0.1 multiply_reduce_fusion
  14.7 4.9 %psum.14 = f32[2,16]{1,0:T(2,128)S(1)} all-reduce(f32[2,16]{1,0:T(2,128)S(1)} %multiply_reduce_fusion), channel_id=1, replica_groups=mesh['pipe'=4,'expert'=4,'tensor'=2] {'tensor'}, use_global_device_ids=true, to_apply=%region_1.0 | all-reduce | flops 32 | bytes 256 | tf_op jit(solution)/shard_map/psum | solution.py:25
  19.6 0.1 mul.87
  19.7 0.1 fusion.9
  19.8 1.8 %gather_fusion = bf16[96,3584]{1,0:T(8,128)(2,1)} fusion(bf16[33,3584]{1,0:T(8,128)(2,1)S(1)} %concatenate.7, s32[1024]{0:T(1024)S(1)} %pad_clamp_fusion.1), kind=kCustom, calls=%fused_computation | custom fusion | bytes 1376640 | tf_op jit(solution)/shard_map/gather | solution.py:51
  21.6 4.9 %all-to-all-start = ((bf16[4,24,3584]{2,1,0:T(8,128)(2,1)}), bf16[4,24,3584]{2,1,0:T(8,128)(2,1)S(1)}, u32[]{:S(2)}, u32[]{:S(2)}) async-start(bf16[4,24,3584]{2,1,0:T(8,128)(2,1)} %bitcast.9), calls=%async_computation | async-start | bytes 1376256 | tf_op jit(solution)/shard_map/all_to_all | solution.py:54
  26.5 17.3 %all-to-all-done = bf16[4,24,3584]{2,1,0:T(8,128)(2,1)S(1)} async-done(((bf16[4,24,3584]{2,1,0:T(8,128)(2,1)}), bf16[4,24,3584]{2,1,0:T(8,128)(2,1)S(1)}, u32[]{:S(2)}, u32[]{:S(2)}) %all-to-all-start) | async-done | bytes 688160 | tf_op jit(solution)/shard_map/all_to_all | solution.py:54
  43.8 5.1 %fusion.2 = f32[96,1024]{1,0:T(8,128)} fusion(bf16[96,3584]{1,0:T(8,128)(2,1)S(1)} %bitcast.62, bf16[1,3584,1024]{2,1,0:T(8,128)(2,1)} %param.10), kind=kOutput, calls=%fused_computation.6 | convolution fusion | flops 704643072 | bytes 8421376 | tf_op jit(solution)/shard_map/dot_general | solution.py:57
  49.0 0.1 copy.11
  49.1 0.1 reshape.139
  49.2 1.8 %fusion.10 = f32[2,16,4]{1,2,0:T(4,128)S(1)} fusion(f32[2,16]{1,0:T(2,128)S(1)} %add_rsqrt_fusion, f32[3584]{0:T(1024)S(1)} %reduce, f32[1,3584,4]{1,2,0:T(4,128)S(1)} %copy-done, bf16[1,16,3584]{2,1,0:T(8,128)(2,1)S(1)} %collective-permute-done.1, bf16[1,16,3584]{2,1,0:T(8,128)(2,1)S(1)} %collective-permute-done), kind=kOutput, calls=%fused_computation.14 | convolution fusion | flops 5963776 | bytes 301696 | tf_op jit(solution)/shard_map/dtc,ce->dte/dot_general | solution.py:28
  51.0 4.9 %psum.15 = f32[2,16,4]{1,2,0:T(4,128)S(1)} all-reduce(f32[2,16,4]{1,2,0:T(4,128)S(1)} %fusion.10), channel_id=1, replica_groups=mesh['pipe'=4,'expert'=4,'tensor'=2] {'tensor'}, use_global_device_ids=true, to_apply=%region_2.0 | all-reduce | flops 128 | bytes 1024 | tf_op jit(solution)/shard_map/psum | solution.py:28
  55.9 1.0 gather_fusion.2
  56.9 0.1 reshape.142
  57.0 0.1 copy.12
  57.1 4.2 %reduce-scatter.2.cloned.1.call-done = f32[96,512]{1,0:T(8,128)} async-done(((f32[96,1024]{1,0:T(8,128)}), f32[96,512]{1,0:T(8,128)}) %reduce-scatter.2.cloned.1.call-update) | async-done | bytes 196624 | tf_op jit(solution)/shard_map/reduce_scatter | solution.py:58
  61.4 1.0 %multiply_convert_fusion = bf16[96,512]{1,0:T(8,128)(2,1)S(1)} fusion(f32[96,512]{1,0:T(8,128)} %reduce-scatter.2.cloned.1.call-done), kind=kLoop, calls=%fused_computation.23 | loop fusion | flops 245760 | bytes 294912 | tf_op jit(solution)/shard_map/convert_element_type | solution.py:59
  62.4 5.3 %all_gather.3 = bf16[96,1024]{1,0:T(8,128)(2,1)S(1)} all-gather(bf16[96,512]{1,0:T(8,128)(2,1)S(1)} %multiply_convert_fusion), channel_id=1, replica_groups=mesh['pipe'=4,'expert'=4,'tensor'=2] {'tensor'}, dimensions={1}, use_global_device_ids=true | all-gather | bytes 294912 | tf_op jit(solution)/shard_map/all_gather | solution.py:59
  67.6 4.4 %fusion.4 = bf16[96,3584]{1,0:T(8,128)(2,1)S(1)} fusion(bf16[96,1024]{1,0:T(8,128)(2,1)S(1)} %all_gather.3, bf16[1,1024,3584]{2,1,0:T(8,128)(2,1)} %param.11), kind=kOutput, calls=%fused_computation.8 | convolution fusion | flops 704987136 | bytes 8224768 | tf_op jit(solution)/shard_map/dot_general | solution.py:60
  72.1 0.1 constant_dynamic-slice_fusion.2
  72.1 1.5 %collective-permute-start.2 = (bf16[1,24,3584]{2,1,0:T(8,128)(2,1)S(1)}, bf16[1,24,3584]{2,1,0:T(8,128)(2,1)S(1)}, u32[]{:S(2)}, u32[]{:S(2)}) collective-permute-start(bf16[1,24,3584]{2,1,0:T(8,128)(2,1)S(1)} %get-tuple-element.9), channel_id=1, source_target_pairs={{0,2},{2,0},{4,6},{6,4},{1,3},{3,1},{5,7},{7,5},{8,10},{10,8},{12,... | collective-permute-start | bytes 516104 | tf_op jit(solution)/shard_map/ppermute | solution.py:72
  73.7 0.1 copy.15
  73.8 2.5 %collective-permute-start.3 = (bf16[1,24,3584]{2,1,0:T(8,128)(2,1)S(1)}, bf16[1,24,3584]{2,1,0:T(8,128)(2,1)S(1)}, u32[]{:S(2)}, u32[]{:S(2)}) collective-permute-start(bf16[1,24,3584]{2,1,0:T(8,128)(2,1)S(1)} %get-tuple-element.8), channel_id=1, source_target_pairs={{0,4},{2,6},{4,0},{6,2},{1,5},{3,7},{5,1},{7,3},{8,12},{10,14},{12... | collective-permute-start | bytes 516104 | tf_op jit(solution)/shard_map/ppermute | solution.py:72
  76.3 0.5 collective-permute-start.4
  76.8 2.8 %collective-permute-done.2 = bf16[1,24,3584]{2,1,0:T(8,128)(2,1)S(1)} collective-permute-done((bf16[1,24,3584]{2,1,0:T(8,128)(2,1)S(1)}, bf16[1,24,3584]{2,1,0:T(8,128)(2,1)S(1)}, u32[]{:S(2)}, u32[]{:S(2)}) %collective-permute-start.2) | collective-permute-done | bytes 172064 | tf_op jit(solution)/shard_map/ppermute | solution.py:72
  79.6 8.8 %collective-permute-done.3 = bf16[1,24,3584]{2,1,0:T(8,128)(2,1)S(1)} collective-permute-done((bf16[1,24,3584]{2,1,0:T(8,128)(2,1)S(1)}, bf16[1,24,3584]{2,1,0:T(8,128)(2,1)S(1)}, u32[]{:S(2)}, u32[]{:S(2)}) %collective-permute-start.3) | collective-permute-done | bytes 172064 | tf_op jit(solution)/shard_map/ppermute | solution.py:72
  88.5 0.8 gather_fusion.1
  89.3 0.2 reshape.121
  89.5 0.6 fusion.27
  90.1 0.7 fusion.14
  (24 shorter events, 0.2 us)
Async XLA Ops:
  6.5 42.7 %copy-start = (f32[1,3584,4]{1,2,0:T(4,128)S(1)}, f32[1,3584,4]{1,2,0:T(4,128)}, u32[]{:S(2)}) copy-start(f32[1,3584,4]{1,2,0:T(4,128)} %param.9) | copy-start | bytes 172036
  7.5 6.6 %collective-permute-start.1 = (bf16[1,16,3584]{2,1,0:T(8,128)(2,1)S(1)}, bf16[1,16,3584]{2,1,0:T(8,128)(2,1)S(1)}, u32[]{:S(2)}, u32[]{:S(2)}) collective-permute-start(bf16[1,16,3584]{2,1,0:T(8,128)(2,1)S(1)} %get-tuple-element.12), channel_id=1, source_target_pairs={{0,24},{8,0},{16,8},{24,16},{1,25},{9,1},{17,9},{25,17},{2,26},{10... | collective-permute-start | bytes 344072 | tf_op jit(solution)/shard_map/ppermute | solution.py:12
  10.0 4.6 %collective-permute-start = (bf16[1,16,3584]{2,1,0:T(8,128)(2,1)S(1)}, bf16[1,16,3584]{2,1,0:T(8,128)(2,1)S(1)}, u32[]{:S(2)}, u32[]{:S(2)}) collective-permute-start(bf16[1,16,3584]{2,1,0:T(8,128)(2,1)S(1)} %get-tuple-element.11), channel_id=1, source_target_pairs={{0,8},{8,16},{16,24},{24,0},{1,9},{9,17},{17,25},{25,1},{2,10},{10... | collective-permute-start | bytes 344072 | tf_op jit(solution)/shard_map/ppermute | solution.py:12
  21.6 22.2 %all-to-all-start = ((bf16[4,24,3584]{2,1,0:T(8,128)(2,1)}), bf16[4,24,3584]{2,1,0:T(8,128)(2,1)S(1)}, u32[]{:S(2)}, u32[]{:S(2)}) async-start(bf16[4,24,3584]{2,1,0:T(8,128)(2,1)} %bitcast.9), calls=%async_computation | async-start | bytes 1376256 | tf_op jit(solution)/shard_map/all_to_all | solution.py:54
  26.5 34.8 %reduce-scatter.2.cloned.1.call-start = ((), (), s32[]{:S(2)}) async-start(), calls=%async_computation.2 | async-start | bytes 589824 | tf_op jit(solution)/shard_map/reduce_scatter | solution.py:58
  43.8 5.2 %copy-start.1 = (s32[2,1,16,2]{2,3,1,0:T(2,128)S(1)}, s32[2,1,16,2]{2,3,1,0:T(2,128)}, u32[]{:S(2)}) copy-start(s32[2,1,16,2]{2,3,1,0:T(2,128)} %param.7) | copy-start | bytes 772
  72.1 7.4 %collective-permute-start.2 = (bf16[1,24,3584]{2,1,0:T(8,128)(2,1)S(1)}, bf16[1,24,3584]{2,1,0:T(8,128)(2,1)S(1)}, u32[]{:S(2)}, u32[]{:S(2)}) collective-permute-start(bf16[1,24,3584]{2,1,0:T(8,128)(2,1)S(1)} %get-tuple-element.9), channel_id=1, source_target_pairs={{0,2},{2,0},{4,6},{6,4},{1,3},{3,1},{5,7},{7,5},{8,10},{10,8},{12,... | collective-permute-start | bytes 516104 | tf_op jit(solution)/shard_map/ppermute | solution.py:72
  73.8 14.6 %collective-permute-start.3 = (bf16[1,24,3584]{2,1,0:T(8,128)(2,1)S(1)}, bf16[1,24,3584]{2,1,0:T(8,128)(2,1)S(1)}, u32[]{:S(2)}, u32[]{:S(2)}) collective-permute-start(bf16[1,24,3584]{2,1,0:T(8,128)(2,1)S(1)} %get-tuple-element.8), channel_id=1, source_target_pairs={{0,4},{2,6},{4,0},{6,2},{1,5},{3,7},{5,1},{7,3},{8,12},{10,14},{12... | collective-permute-start | bytes 516104 | tf_op jit(solution)/shard_map/ppermute | solution.py:72
  76.3 12.2 %collective-permute-start.4 = (bf16[1,24,3584]{2,1,0:T(8,128)(2,1)S(1)}, bf16[1,24,3584]{2,1,0:T(8,128)(2,1)S(1)}, u32[]{:S(2)}, u32[]{:S(2)}) collective-permute-start(bf16[1,24,3584]{2,1,0:T(8,128)(2,1)S(1)} %get-tuple-element.7), channel_id=1, source_target_pairs={{0,6},{2,4},{4,2},{6,0},{1,7},{3,5},{5,3},{7,1},{8,14},{10,12},{12... | collective-permute-start | bytes 516104 | tf_op jit(solution)/shard_map/ppermute | solution.py:72
Sparse Core Ops, SparseCore 0:
  49.1 12.2 reduce-scatter.1
